TPU v7x, 768 devices: a whole 4x8x12 slice. The times are simulated.
768 devices in a mesh: dp: 96 (over x, z, core), section: 8 (over y).
Axes of the slice: x: 4, y: 8, z: 12, core: 2. Of those that a mesh axis runs over, the one named last changes fastest.
Arguments:
- weights: bfloat16 [8, 6144, 256], P('section'), may hold values from -0.125 to 0.125
- inputs: bfloat16 [8, 49152, 2048], P('section', 'dp'), may hold values from -40 to 40
- out_grads: bfloat16 [8, 49152, 2048], P('section', 'dp'), may hold values from -40 to 40
- master: float32 [8, 6144, 256], P('section', 'dp'), may hold values from -0.125 to 0.125
- moment1: float32 [8, 6144, 256], P('section', 'dp'), may hold values from -6 to 6
- moment2: float32 [8, 6144, 256], P('section', 'dp'), may hold values from 0.1 to 10
Outputs:
- new_master: float32 [8, 6144, 256], P('section', 'dp')
- new_moment1: float32 [8, 6144, 256], P('section', 'dp')
- new_moment2: float32 [8, 6144, 256], P('section', 'dp')
- new_weights: bfloat16 [8, 6144, 256], P('section')
All inputs are finite; a program needn't handle non-finite values.
Results may differ from a plain program's by a relative error of at most 0.001.
Values may be sent and summed in bfloat16 or wider, within the bound.
A program may use at most 64 MiB of HBM per device.

v0:
```python
import jax
import jax.numpy as jnp
from jax import lax
from jax.sharding import Mesh
from jax.sharding import PartitionSpec as P

MROWS = 256
MICRO = 2
STEP = 10
DP = ("dp_0", "dp_1", "dp_2")
DP_SECTION = ("dp_0", "dp_1", "dp_2", "section")


def sum_in_order(blocks, axes, sequence):
    inside = blocks.shape[1:]
    blocks = blocks.reshape(*(lax.axis_size(a) for a in axes), *inside)
    blocks = jnp.moveaxis(blocks, sequence, range(len(axes))).reshape(-1, *inside)
    for k in sequence:
        blocks = lax.psum_scatter(blocks, axes[k], scatter_dimension=0, tiled=True)
    return blocks[0]


def in_blocks(value, dim, size):
    shape = value.shape
    blocks = value.reshape(*shape[:dim], size, shape[dim] // size, *shape[dim + 1 :])
    return jnp.moveaxis(blocks, dim, 0)


def scatter_axes(value, axes, sequence, dim):
    size = lax.axis_size(axes)
    return sum_in_order(in_blocks(value, dim, size), axes, sequence)


def by_axis(value, axes):
    for axis in axes:
        value = lax.psum(value, axis)
    return value


def in_order(blocks, dim):
    shape = list(blocks.shape[1:])
    shape[dim] *= blocks.shape[0]
    return jnp.moveaxis(blocks, 0, dim).reshape(shape)


def gather_in_order(value, axes, sequence):
    blocks = value
    for k in sequence:
        blocks = lax.all_gather(blocks, axes[k])
    done = sequence[::-1]
    back = [done.index(k) for k in range(len(axes))]
    blocks = blocks.transpose(*back, *range(len(axes), blocks.ndim))
    return blocks.reshape(-1, *value.shape)


def gathered_by_axis(value, axes, sequence, dim):
    return in_order(gather_in_order(value, axes, sequence), dim)


def forward_pieces(x_rows, dy_rows, w_gate, w_up, w_down):
    pre_gate = jnp.dot(x_rows, w_gate, preferred_element_type=jnp.float32)
    pre_up = jnp.dot(x_rows, w_up, preferred_element_type=jnp.float32)
    sigma = jax.nn.sigmoid(pre_gate)
    silu_val = pre_gate * sigma
    hidden = (silu_val * pre_up).astype(jnp.bfloat16)
    d_hidden = jnp.dot(dy_rows, w_down, preferred_element_type=jnp.float32)
    d_gate = (d_hidden * pre_up * sigma * (1.0 + pre_gate * (1.0 - sigma))).astype(jnp.bfloat16)
    d_up = (d_hidden * silu_val).astype(jnp.bfloat16)
    return (d_gate, d_up, hidden)


def block_grads(x_rows, dy_rows, w_gate, w_up, w_down):
    d_gate, d_up, hidden = forward_pieces(x_rows, dy_rows, w_gate, w_up, w_down)
    g_gate = jnp.dot(x_rows.T, d_gate, preferred_element_type=jnp.float32)
    g_up = jnp.dot(x_rows.T, d_up, preferred_element_type=jnp.float32)
    g_down = jnp.dot(dy_rows.T, hidden, preferred_element_type=jnp.float32)
    return jnp.concatenate([g_gate, g_up, g_down], axis=0)


def local(weights, inputs, out_grads, master, moment1, moment2):
    stacked = weights[0]
    width = stacked.shape[0] // 3
    hidden_width = stacked.shape[1]
    w_gate = stacked[:width]
    w_up = stacked[width : 2 * width]
    w_down = stacked[2 * width :]
    local_grad = jnp.zeros(stacked.shape, jnp.float32)
    for micro in range(MICRO):
        x_rows = inputs[0, micro * MROWS : (micro + 1) * MROWS]
        dy_rows = out_grads[0, micro * MROWS : (micro + 1) * MROWS]
        local_grad = local_grad + block_grads(x_rows, dy_rows, w_gate, w_up, w_down)
    shard = scatter_axes(local_grad, DP, (2, 0, 1), 0)
    squares = jnp.sum(shard * shard)
    total = by_axis(squares, DP_SECTION)
    max_norm = jnp.sqrt(jnp.float32(lax.axis_size("section") * 3 * width * hidden_width))
    clip = jnp.minimum(jnp.float32(1.0), max_norm / (jnp.sqrt(total) + 1e-06))
    clipped = clip * shard
    old_param = master[0]
    new_first = 0.9 * moment1[0] + 0.1 * clipped
    new_second = 0.95 * moment2[0] + 0.05 * clipped * clipped
    first_fix = 1.0 - 0.9**STEP
    second_fix = 1.0 - 0.95**STEP
    update = new_first / first_fix / (jnp.sqrt(new_second / second_fix) + 1e-08) + 0.1 * old_param
    new_param = old_param - 0.01 * update
    gathered = gathered_by_axis(new_param.astype(jnp.bfloat16), DP, (0, 1, 2), 0)
    return (new_param[None], new_first[None], new_second[None], gathered[None])


def solution(mesh):
    split = Mesh(
        mesh.devices.reshape(4, 12, 2, mesh.shape["section"]), ("dp_0", "dp_1", "dp_2", "section")
    )
    in_specs = (
        P("section", None, None),
        P("section", DP, None),
        P("section", DP, None),
        P("section", DP, None),
        P("section", DP, None),
        P("section", DP, None),
    )
    out_specs = (
        P("section", DP, None),
        P("section", DP, None),
        P("section", DP, None),
        P("section", None, None),
    )
    return jax.shard_map(local, mesh=split, in_specs=in_specs, out_specs=out_specs, check_vma=False)
```

profile of v0, /device:TPU:1, one launch (start us, length us, event | category | flops | bytes accessed | tf_op | source)
XLA Modules:
  0.0 338.7 jit_solution(12156209382762030605)
XLA Ops:
  7.2 0.0 copy-start
  7.2 0.0 reduce-scatter.4.cloned.1.call-start
  7.2 2.1 fusion.2
  9.3 0.0 copy-done
  9.4 0.0 copy-start.1
  9.4 1.8 fusion.10
  11.2 0.1 copy-done.1
  11.3 0.0 copy-start.5
  11.3 1.8 fusion.7
  13.1 0.4 copy-done.5
  13.5 0.4 fusion.20
  13.9 0.4 fusion.4
  14.4 0.4 fusion.13
  14.8 0.5 convolution_bitcast_fusion.3
  15.3 0.5 convolution_bitcast_fusion.5
  15.8 0.5 convolution_bitcast_fusion.4
  16.3 0.5 convolution_bitcast_fusion
  16.8 0.5 convolution_bitcast_fusion.2
  17.4 0.5 convolution_bitcast_fusion.1
  17.8 3.0 maximum_add_fusion
  20.9 6.6 %copy.15 = f32[6144,256]{1,0:T(8,128)} copy(f32[6144,256]{0,1:T(8,128)} %maximum_add_fusion) | data formatting | bytes 12582912 | tf_op jit(solution)/shard_map/add | solution.py:91
  27.5 6.2 %copy.16 = f32[2,4,12,64,256]{4,3,2,1,0:T(8,128)} copy(f32[2,4,12,64,256]{4,3,0,2,1:T(8,128)} %bitcast.65) | data formatting | bytes 12582912 | tf_op jit(solution)/shard_map/transpose | solution.py:17
  33.7 0.0 reduce-scatter.4.cloned.1.call-update
  33.7 0.0 copy-start.2
  33.7 0.0 copy-start.3
  33.7 0.0 copy-start.4
  33.8 0.0 reduce-scatter.6.cloned.1.call-start
  33.8 33.8 %reduce-scatter.4.cloned.1.call-done = f32[48,64,256]{2,1,0:T(8,128)} async-done(((f32[96,64,256]{2,1,0:T(8,128)}), f32[48,64,256]{2,1,0:T(8,128)}) %reduce-scatter.4.cloned.1.call-update) | async-done | bytes 3145744 | tf_op jit(solution)/shard_map/reduce_scatter | solution.py:19
  67.6 0.0 reduce-scatter.6.cloned.1.call-update
  67.6 0.0 reduce-scatter.8.cloned.1.call-start
  67.6 50.4 %reduce-scatter.6.cloned.1.call-done = f32[12,64,256]{2,1,0:T(8,128)} async-done(((f32[48,64,256]{2,1,0:T(8,128)}), f32[12,64,256]{2,1,0:T(8,128)}) %reduce-scatter.6.cloned.1.call-update) | async-done | bytes 786448 | tf_op jit(solution)/shard_map/reduce_scatter | solution.py:19
  118.0 0.0 reduce-scatter.8.cloned.1.call-update
  118.0 0.0 all-gather.5.cloned.1.call-start
  118.1 53.4 %reduce-scatter.8.cloned.1.call-done = f32[1,64,256]{2,1,0:T(8,128)} async-done(((f32[12,64,256]{2,1,0:T(8,128)}), f32[1,64,256]{2,1,0:T(8,128)}) %reduce-scatter.8.cloned.1.call-update) | async-done | bytes 65552 | tf_op jit(solution)/shard_map/reduce_scatter | solution.py:19
  171.5 1.5 multiply_reduce_fusion
  173.0 9.3 %psum.28 = f32[]{:T(128)} all-reduce(f32[]{:T(128)} %multiply_reduce_fusion), channel_id=1, replica_groups=mesh['dp_0'=4,'dp_1'=12,'dp_2'=2,'section'=8] {'dp_0'}, use_global_device_ids=true, to_apply=%region_4.0 | all-reduce | flops 1 | bytes 8 | tf_op jit(solution)/shard_map/psum | solution.py:36
  182.3 17.5 %psum.29 = f32[]{:T(128)} all-reduce(f32[]{:T(128)} %psum.28), channel_id=1, replica_groups=mesh['dp_0'=4,'dp_1'=12,'dp_2'=2,'section'=8] {'dp_1'}, use_global_device_ids=true, to_apply=%region_5.0 | all-reduce | flops 1 | bytes 8 | tf_op jit(solution)/shard_map/psum | solution.py:36
  199.8 18.0 %psum.30 = f32[]{:T(128)} all-reduce(f32[]{:T(128)} %psum.29), channel_id=1, replica_groups=mesh['dp_0'=4,'dp_1'=12,'dp_2'=2,'section'=8] {'dp_2'}, use_global_device_ids=true, to_apply=%region_6.0 | all-reduce | flops 1 | bytes 8 | tf_op jit(solution)/shard_map/psum | solution.py:36
  217.8 14.1 %psum.31 = f32[]{:T(128)} all-reduce(f32[]{:T(128)} %psum.30), channel_id=1, replica_groups=mesh['dp_0'=4,'dp_1'=12,'dp_2'=2,'section'=8] {'section'}, use_global_device_ids=true, to_apply=%region_7.0 | all-reduce | flops 1 | bytes 8 | tf_op jit(solution)/shard_map/psum | solution.py:36
  232.7 0.0 copy-done.2
  232.7 0.0 copy-done.3
  232.7 0.0 copy-done.4
  232.7 1.5 fusion.57
  234.2 10.3 %all_gather.16 = bf16[4,64,256]{2,1,0:T(8,128)(2,1)} all-gather(bf16[1,64,256]{2,1,0:T(8,128)(2,1)S(1)} %get-tuple-element.4), channel_id=1, replica_groups=mesh['dp_0'=4,'dp_1'=12,'dp_2'=2,'section'=8] {'dp_0'}, dimensions={0}, use_global_device_ids=true | all-gather | bytes 163840 | tf_op jit(solution)/shard_map/all_gather | solution.py:49
  244.5 0.0 all-gather.5.cloned.1.call-update
  244.5 0.0 all-gather.7.cloned.1.call-start
  244.6 52.6 %all-gather.5.cloned.1.call-done = bf16[48,64,256]{2,1,0:T(8,128)(2,1)} async-done(((bf16[4,64,256]{2,1,0:T(8,128)(2,1)}), bf16[48,64,256]{2,1,0:T(8,128)(2,1)}) %all-gather.5.cloned.1.call-update) | async-done | bytes 1572880 | tf_op jit(solution)/shard_map/all_gather | solution.py:49
  297.2 0.0 all-gather.7.cloned.1.call-update
  297.2 31.0 %all-gather.7.cloned.1.call-done = bf16[24,4,64,256]{3,2,1,0:T(8,128)(2,1)} async-done(((bf16[12,4,64,256]{3,2,1,0:T(8,128)(2,1)}), bf16[24,4,64,256]{3,2,1,0:T(8,128)(2,1)}) %all-gather.7.cloned.1.call-update) | async-done | bytes 3145744 | tf_op jit(solution)/shard_map/all_gather | solution.py:49
  328.2 4.0 %copy.17 = bf16[4,12,2,64,256]{4,3,2,1,0:T(8,128)(2,1)} copy(bf16[4,12,2,64,256]{4,3,0,1,2:T(8,128)(2,1)} %bitcast.67) | data formatting | bytes 6291456 | tf_op jit(solution)/shard_map/transpose | solution.py:52
Async XLA Ops:
  7.2 2.2 copy-start
  7.2 60.4 %reduce-scatter.4.cloned.1.call-start = ((), (), s32[]{:S(2)}) async-start(), calls=%async_computation.3 | async-start | bytes 9437184 | tf_op jit(solution)/shard_map/reduce_scatter | solution.py:19
  9.4 1.9 copy-start.1
  11.3 2.2 copy-start.5
  33.7 198.9 %copy-start.2 = (f32[1,64,256]{2,1,0:T(8,128)S(1)}, f32[1,64,256]{2,1,0:T(8,128)}, u32[]{:S(2)}) copy-start(f32[1,64,256]{2,1,0:T(8,128)} %param.9) | copy-start | bytes 196612
  33.7 198.9 %copy-start.3 = (f32[1,64,256]{2,1,0:T(8,128)S(1)}, f32[1,64,256]{2,1,0:T(8,128)}, u32[]{:S(2)}) copy-start(f32[1,64,256]{2,1,0:T(8,128)} %param.10) | copy-start | bytes 196612
  33.7 198.9 %copy-start.4 = (f32[1,64,256]{2,1,0:T(8,128)S(1)}, f32[1,64,256]{2,1,0:T(8,128)}, u32[]{:S(2)}) copy-start(f32[1,64,256]{2,1,0:T(8,128)} %param.11) | copy-start | bytes 196612
  33.8 84.2 %reduce-scatter.6.cloned.1.call-start = ((), (), s32[]{:S(2)}) async-start(), calls=%async_computation.4 | async-start | bytes 3932160 | tf_op jit(solution)/shard_map/reduce_scatter | solution.py:19
  67.6 103.9 %reduce-scatter.8.cloned.1.call-start = ((), (), s32[]{:S(2)}) async-start(), calls=%async_computation.5 | async-start | bytes 851968 | tf_op jit(solution)/shard_map/reduce_scatter | solution.py:19
  118.0 179.1 %all-gather.5.cloned.1.call-start = ((), (), s32[]{:S(2)}) async-start(), calls=%async_computation.6 | async-start | bytes 1703936 | tf_op jit(solution)/shard_map/all_gather | solution.py:49
  244.5 83.6 %all-gather.7.cloned.1.call-start = ((), (), s32[]{:S(2)}) async-start(), calls=%async_computation.7 | async-start | bytes 4718592 | tf_op jit(solution)/shard_map/all_gather | solution.py:49
Sparse Core Ops, SparseCore 0:
  33.8 33.6 reduce-scatter.3
  70.7 47.2 reduce-scatter.5
  121.1 50.3 reduce-scatter.7
  244.7 52.4 all-gather.4
  299.4 28.7 all-gather.6
where the time goes:
time: 339 us
  waiting for transfers between devices  221 us (65%)
  blocking collectives  69.2 us (20%)
  local copies, waits for them, and re-layouts  17.4 us (5%)
  between operations  14.6 us (4%)
  matrix products  10 us (3%)
  other arithmetic  6 us (2%)
    reduce_scatter x3, waiting for transfers between devices, sum_in_order(): blocks = lax.psum_scatter(blocks, axes[k], scatter_dimension=0, tiled=True)  138 us
    all_gather x2, waiting for transfers between devices, gather_in_order(): blocks = lax.all_gather(blocks, axes[k])  83.5 us
    psum x4, blocking collectives, by_axis(): value = lax.psum(value, axis)  58.9 us
    all_gather x1, blocking collectives, gather_in_order(): blocks = lax.all_gather(blocks, axes[k])  10.3 us
  transfers between devices with their start and end apart: 5, of which 5 were waited for; matrix products, arithmetic and copies ran while one was open for 0% of the time, Pallas kernels for 0%

commit v1 on v0

v1 whole, which is shorter than its diff:
```python
import functools

import jax
import jax.numpy as jnp
from jax import lax
from jax.experimental import pallas as pl
from jax.experimental.pallas import tpu as pltpu
from jax.sharding import Mesh
from jax.sharding import PartitionSpec as P

STEP = 10
NX, NZ, NC, NY = 4, 12, 2, 8
ROWS = 64
WIDTH = 256
DP = ("dp_0", "dp_1", "dp_2")
MESH = pl.DeviceIdType.MESH
HALVES = (pl.ds(0, 32), pl.ds(32, 32))
REDUCE_ORDER = (6, 5, -5, 4, -4, 3, -3, 2, -2, 1, -1, 0)
GATHER_ORDER = (0, -1, 1, -2, 2, -3, 3, -4, 4, -5, 5, 6)


def grads_kernel(w_ref, x_ref, dy_ref, keep_ref, give_ref, a_ref, b_ref, dh_ref, d_ref):
    core = lax.axis_index("dp_2")
    depth = x_ref.shape[1]
    f32 = jnp.float32
    a_ref[...] = jnp.dot(x_ref[...], w_ref[0:depth], preferred_element_type=f32)
    b_ref[...] = jnp.dot(x_ref[...], w_ref[depth : 2 * depth], preferred_element_type=f32)
    dh_ref[...] = jnp.dot(dy_ref[...], w_ref[2 * depth :], preferred_element_type=f32)
    for r in range(0, x_ref.shape[0], 128):
        rows = pl.ds(r, 128)
        a, b, dh = a_ref[rows], b_ref[rows], dh_ref[rows]
        sigma = jax.nn.sigmoid(a)
        silu = a * sigma
        d_ref[0, rows] = (dh * b * sigma * (1.0 + a * (1.0 - sigma))).astype(jnp.bfloat16)
        d_ref[1, rows] = (dh * silu).astype(jnp.bfloat16)
        d_ref[2, rows] = (silu * b).astype(jnp.bfloat16)
    first = core == 0
    for part in range(3):
        rows_ref = dy_ref if part == 2 else x_ref
        for j in range(0, depth, 512):
            p = lax.dot_general(
                rows_ref[:, j : j + 512], d_ref[part], (((0,), (0,)), ((), ())), preferred_element_type=f32
            )
            for k in range(0, 512, 128):
                block = (part * depth + j + k) // 128
                low, high = p[k : k + 64], p[k + 64 : k + 128]
                keep_ref[block // NZ, block % NZ] = jnp.where(first, low, high)
                give_ref[block // NZ, block % NZ] = jnp.where(first, high, low).astype(jnp.bfloat16)


def local_grads(weights, x_rows, dy_rows):
    tokens = x_rows.shape[0]
    vmem = pl.BlockSpec(memory_space=pltpu.VMEM)
    return pl.pallas_call(
        grads_kernel,
        out_shape=(
            jax.ShapeDtypeStruct((NX, NZ, ROWS, WIDTH), jnp.float32),
            jax.ShapeDtypeStruct((NX, NZ, ROWS, WIDTH), jnp.bfloat16),
        ),
        in_specs=[vmem] * 3,
        out_specs=(vmem, vmem),
        scratch_shapes=[
            pltpu.VMEM((tokens, WIDTH), jnp.float32),
            pltpu.VMEM((tokens, WIDTH), jnp.float32),
            pltpu.VMEM((tokens, WIDTH), jnp.float32),
            pltpu.VMEM((3, tokens, WIDTH), jnp.bfloat16),
        ],
        compiler_params=pltpu.CompilerParams(vmem_limit_bytes=32 << 20),
    )(weights, x_rows, dy_rows)


def step_kernel(
    keep_ref, give_ref, master_ref, m1_ref, m2_ref,
    new_master_ref, new_m1_ref, new_m2_ref, all_ref,
    pair_buf, x1_out, x1_left, x1_right, x2_outr, x2_outl, x2_left, x2_right,
    zp_out, zm_out, zp_in, zm_in, norm_out, norm_in,
    pair_s, pair_r, x1_s, x1_r, x2_s, x2_r, z_s, z_r, n_s, n_r, gz_s, gz_r, gx_s, gx_r, gp_s, gp_r,
):
    f32, bf16 = jnp.float32, jnp.bfloat16
    mx, mz, mc, my = (lax.axis_index(n) for n in ("dp_0", "dp_1", "dp_2", "section"))

    def to_x(k):
        return {"dp_0": lax.rem(mx + (k + NX), NX)}

    def to_z(k):
        return {"dp_1": lax.rem(mz + (k + NZ), NZ)}

    def to_y(k):
        return {"section": lax.rem(my + (k + NY), NY)}

    partner = {"dp_2": 1 - mc}
    peers = [partner]
    peers += [to_x(k) for k in range(1, NX)]
    peers += [to_z(k) for k in range(1, NZ)]
    peers += [to_y(k) for k in range(1, NY)]
    barrier = pltpu.get_barrier_semaphore()
    for peer in peers:
        pl.semaphore_signal(barrier, inc=1, device_id=peer, device_id_type=MESH)
    pl.semaphore_wait(barrier, len(peers))

    started = []

    def send(src, dst, s, r, device):
        copy = pltpu.make_async_remote_copy(
            src_ref=src, dst_ref=dst, send_sem=s, recv_sem=r, device_id=device, device_id_type=MESH
        )
        copy.start()
        started.append(copy)
        return copy

    def xi(k):
        return lax.rem(mx + (k + NX), NX)

    def zi(k):
        return lax.rem(mz + (k + NZ), NZ)

    pair = {}
    for g, off in enumerate(REDUCE_ORDER):
        pair[g] = send(give_ref.at[:, zi(off)], pair_buf.at[g], pair_s.at[g], pair_r.at[g], partner)

    x1, x2, zc = {}, {}, {}

    def own(g, k):
        x = xi(k)
        return keep_ref[x, zi(REDUCE_ORDER[g])] + pair_buf[g, x].astype(f32)

    def first_x(g):
        pair[g].wait_recv()
        x1_out[g] = own(g, 2).astype(bf16)
        x1[g, 0] = send(x1_out.at[g, HALVES[0]], x1_left.at[g], x1_s.at[0, g], x1_r.at[0, g], to_x(1))
        x1[g, 1] = send(x1_out.at[g, HALVES[1]], x1_right.at[g], x1_s.at[1, g], x1_r.at[1, g], to_x(-1))

    def second_x(g):
        right, left = own(g, 1), own(g, -1)
        x1[g, 0].wait_recv()
        x2_outr[g, 0:32] = (right[:32] + x1_left[g].astype(f32)).astype(bf16)
        x2_outr[g, 32:64] = right[32:].astype(bf16)
        x2[g, 0] = send(x2_outr.at[g], x2_left.at[g], x2_s.at[0, g], x2_r.at[0, g], to_x(1))
        x1[g, 1].wait_recv()
        x2_outl[g, 0:32] = left[:32].astype(bf16)
        x2_outl[g, 32:64] = (left[32:] + x1_right[g].astype(f32)).astype(bf16)
        x2[g, 1] = send(x2_outl.at[g], x2_right.at[g], x2_s.at[1, g], x2_r.at[1, g], to_x(-1))

    def pass_z(way, dist, reduced):
        out, arrived = ((zp_out, zp_in), (zm_out, zm_in))[way]
        for sub, rows in enumerate(HALVES):
            if dist == 6 and sub != way:
                continue
            value = reduced[32 * sub : 32 * sub + 32]
            if dist < 5 or (dist == 5 and sub == way):
                zc[way, dist, sub].wait_recv()
                value = value + arrived[dist, rows]
            out[dist - 1, rows] = value
            zc[way, dist - 1, sub] = send(
                out.at[dist - 1, rows], arrived.at[dist - 1, rows],
                z_s.at[way, dist - 1, sub], z_r.at[way, dist - 1, sub], to_z(1 - 2 * way),
            )

    def third_x(g):
        off = REDUCE_ORDER[g]
        mine = own(g, 0)
        x2[g, 0].wait_recv()
        x2[g, 1].wait_recv()
        reduced = mine + x2_left[g].astype(f32) + x2_right[g].astype(f32)
        if off == 6:
            pass_z(0, 6, reduced)
            pass_z(1, 6, reduced)
        elif off > 0:
            pass_z(0, off, reduced)
        elif off < 0:
            pass_z(1, -off, reduced)
        return reduced

    lag = 2
    count = len(REDUCE_ORDER)
    reduced = None
    for t in range(count + 2 * lag):
        if t < count:
            first_x(t)
        if 0 <= t - lag < count:
            second_x(t - lag)
        if 0 <= t - 2 * lag < count:
            reduced = third_x(t - 2 * lag)
    for way in range(2):
        for sub in range(2):
            zc[way, 0, sub].wait_recv()
    grad = reduced + zp_in[0] + zm_in[0]

    squares = grad * grad
    part = squares[0:8]
    for k in range(8, ROWS, 8):
        part = part + squares[k : k + 8]
    part = part[:, :128] + part[:, 128:]
    slot = 0
    stages = (
        [partner],
        [to_z(k) for k in range(1, NZ)],
        [to_x(k) for k in range(1, NX)],
        [to_y(k) for k in range(1, NY)],
    )
    for stage, devices in enumerate(stages):
        norm_out[stage] = part
        copies = []
        for device in devices:
            copies.append(send(norm_out.at[stage], norm_in.at[slot], n_s.at[slot], n_r.at[slot], device))
            slot += 1
        for k, copy in enumerate(copies):
            copy.wait_recv()
            part = part + norm_in[slot - len(copies) + k]
    total = jnp.sum(part, axis=(0, 1), keepdims=True)
    max_norm = jnp.sqrt(jnp.full((1, 1), float(NY * NX * NZ * NC * ROWS * WIDTH), f32))
    clip = jnp.minimum(1.0, max_norm / (jnp.sqrt(total) + 1e-06))
    clipped = clip * grad
    master = master_ref[...]
    new_m1 = 0.9 * m1_ref[...] + 0.1 * clipped
    new_m2 = 0.95 * m2_ref[...] + 0.05 * clipped * clipped
    update = new_m1 / (1.0 - 0.9**STEP) / (jnp.sqrt(new_m2 / (1.0 - 0.95**STEP)) + 1e-08) + 0.1 * master
    new_master = master - 0.01 * update
    new_m1_ref[...] = new_m1
    new_m2_ref[...] = new_m2
    new_master_ref[...] = new_master
    all_ref[mx, mz, mc] = new_master.astype(bf16)

    gz, gx, gr, gp = {}, {}, {}, {}

    def block(k, off, rows=None):
        ref = all_ref.at[xi(k), zi(off), mc]
        return ref if rows is None else ref.at[rows]

    def to_partner(g, j, k, off):
        ref = block(k, off)
        gp[g, j] = send(ref, ref, gp_s.at[g, j], gp_r.at[g, j], partner)

    def pass_on_z(way, dist, off):
        if dist > 5:
            return
        ref = block(0, off, HALVES[way] if dist == 5 else None)
        gz[way, dist] = send(ref, ref, gz_s.at[way, dist], gz_r.at[way, dist], to_z(1 - 2 * way))

    def gather_z(g):
        off = GATHER_ORDER[g]
        if off == 0:
            pass_on_z(0, 0, 0)
            pass_on_z(1, 0, 0)
        elif off == 6:
            gz[0, 5].wait_recv()
            gz[1, 5].wait_recv()
        else:
            way, dist = (0, -off) if off < 0 else (1, off)
            gz[way, dist - 1].wait_recv()
            pass_on_z(way, dist, off)
        ref = block(0, off)
        gx[g, 0] = send(ref, ref, gx_s.at[0, g], gx_r.at[0, g], to_x(1))
        gx[g, 1] = send(ref, ref, gx_s.at[1, g], gx_r.at[1, g], to_x(-1))
        to_partner(g, 0, 0, off)

    def gather_x(g):
        off = GATHER_ORDER[g]
        for way in range(2):
            gx[g, way].wait_recv()
            k = 2 * way - 1
            ref = block(k, off, HALVES[way])
            gr[g, way] = send(ref, ref, gx_s.at[2 + way, g], gx_r.at[2 + way, g], to_x(-k))
            to_partner(g, 1 + way, k, off)

    def gather_far(g):
        gr[g, 0].wait_recv()
        gr[g, 1].wait_recv()
        to_partner(g, 3, 2, GATHER_ORDER[g])

    for t in range(count + 2 * lag):
        if t < count:
            gather_z(t)
        if 0 <= t - lag < count:
            gather_x(t - lag)
        if 0 <= t - 2 * lag < count:
            gather_far(t - 2 * lag)
    for copy in gp.values():
        copy.wait_recv()
    for copy in started:
        copy.wait_send()


def reduce_step_gather(keep, give, master, m1, m2):
    f32, bf16 = jnp.float32, jnp.bfloat16
    vmem = pl.BlockSpec(memory_space=pltpu.VMEM)
    state = jax.ShapeDtypeStruct((ROWS, WIDTH), f32)
    dma = pltpu.SemaphoreType.DMA
    wide = pltpu.VMEM((NZ, ROWS, WIDTH), bf16)
    half = pltpu.VMEM((NZ, ROWS // 2, WIDTH), bf16)
    ring = pltpu.VMEM((6, ROWS, WIDTH), f32)
    peers = 1 + (NX - 1) + (NZ - 1) + (NY - 1)
    return pl.pallas_call(
        step_kernel,
        out_shape=(state, state, state, jax.ShapeDtypeStruct((NX, NZ, NC, ROWS, WIDTH), bf16)),
        in_specs=[vmem] * 5,
        out_specs=(vmem,) * 4,
        scratch_shapes=[
            pltpu.VMEM((NZ, NX, ROWS, WIDTH), bf16),
            wide, half, half, wide, wide, wide, wide,
            ring, ring, ring, ring,
            pltpu.VMEM((4, 8, 128), f32),
            pltpu.VMEM((peers, 8, 128), f32),
            dma((NZ,)), dma((NZ,)),
            dma((2, NZ)), dma((2, NZ)),
            dma((2, NZ)), dma((2, NZ)),
            dma((2, 6, 2)), dma((2, 6, 2)),
            dma((peers,)), dma((peers,)),
            dma((2, 6)), dma((2, 6)),
            dma((4, NZ)), dma((4, NZ)),
            dma((NZ, 4)), dma((NZ, 4)),
        ],
        compiler_params=pltpu.CompilerParams(
            collective_id=0, has_side_effects=True, vmem_limit_bytes=40 << 20
        ),
    )(keep, give, master, m1, m2)


def local(weights, inputs, out_grads, master, moment1, moment2):
    keep, give = local_grads(weights[0], inputs[0], out_grads[0])
    new_master, new_m1, new_m2, gathered = reduce_step_gather(keep, give, master[0], moment1[0], moment2[0])
    return (new_master[None], new_m1[None], new_m2[None], gathered.reshape(weights.shape))


def solution(mesh):
    split = Mesh(
        mesh.devices.reshape(NX, NZ, NC, mesh.shape["section"]), ("dp_0", "dp_1", "dp_2", "section")
    )
    shard = P("section", DP, None)
    whole = P("section", None, None)
    return jax.shard_map(
        local,
        mesh=split,
        in_specs=(whole, shard, shard, shard, shard, shard),
        out_specs=(shard, shard, shard, whole),
        check_vma=False,
    )
```

time: 339 us -> 108 us (0.32)
  waiting for transfers between devices: 221 us -> 0 us
  Pallas kernels: 0 us -> 98.8 us
  blocking collectives: 69.2 us -> 0 us
  between operations: 14.6 us -> 0.69 us
  matrix products: 10 us -> 0 us
  local copies, waits for them, and re-layouts: 17.4 us -> 8.63 us
  other arithmetic: 6 us -> 0 us
    reduce_scatter x3 -> x0, waiting for transfers between devices: 138 us -> none  [sum_in_order(): blocks = lax.psum_scatter(blocks, axes[k], scatter_dimension=0, tiled=True)]
    pallas_call x0 -> x2, Pallas kernels: none -> 98.8 us  [the longest x1 94.1 us: reduce_step_gather(): pl.pallas_call(step_kernel, out_shape=(state, state, state, jax.ShapeDtyp...]
    all_gather x2 -> x0, waiting for transfers between devices: 83.5 us -> none  [gather_in_order(): blocks = lax.all_gather(blocks, axes[k])]
    psum x4 -> x0, blocking collectives: 58.9 us -> none  [by_axis(): value = lax.psum(value, axis)]
    all_gather x1 -> x0, blocking collectives: 10.3 us -> none  [gather_in_order(): blocks = lax.all_gather(blocks, axes[k])]
    transpose x2 -> x0, local copies, waits for them, and re-layouts: 10.2 us -> none  [the longest x1 6.25 us: sum_in_order(): jnp.moveaxis(blocks, sequence, range(len(axes))).reshape(-1, *inside)]
    dot_general x12 -> x0, matrix products: 10 us -> none  [the longest x2 3.92 us: forward_pieces(): pre_gate = jnp.dot(x_rows, w_gate, preferred_element_type=jnp.float32)]
    unnamed x12 -> x16, local copies, waits for them, and re-layouts: 0.55 us -> 8.63 us
  transfers between devices with their start and end apart: 5 -> 0, of which waited for: 5 -> 0; matrix products, arithmetic and copies ran while one was open for 0% -> 0% of each run, Pallas kernels for 0% -> 0%
where the time goes in v1:
time: 108 us
  Pallas kernels  98.8 us (91%)
  local copies, waits for them, and re-layouts  8.63 us (8%)
    pallas_call x1, Pallas kernels, reduce_step_gather(): pl.pallas_call(step_kernel, out_shape=(state, state, state, jax.ShapeDtyp...  94.1 us
    unnamed x16, local copies, waits for them, and re-layouts  8.63 us
    pallas_call x1, Pallas kernels, local_grads(): pl.pallas_call(grads_kernel, out_shape=(jax.ShapeDtypeStruct((NX, NZ, ROW...  4.64 us

profile of v1, /device:TPU:1, one launch (start us, length us, event | category | flops | bytes accessed | tf_op | source)
XLA Modules:
  0.0 108.1 jit_solution(3730208184286914171)
XLA Ops:
  0.6 0.0 copy-start
  0.6 1.9 %copy-done = bf16[1,6144,256]{2,1,0:T(8,128)(2,1)S(1)} copy-done((bf16[1,6144,256]{2,1,0:T(8,128)(2,1)S(1)}, bf16[1,6144,256]{2,1,0:T(8,128)(2,1)}, u32[]{:S(2)}) %copy-start) | copy-done | bytes 3145752
  2.5 0.0 copy-start.1
  2.5 1.6 %copy-done.1 = bf16[1,512,2048]{2,1,0:T(8,128)(2,1)S(1)} copy-done((bf16[1,512,2048]{2,1,0:T(8,128)(2,1)S(1)}, bf16[1,512,2048]{2,1,0:T(8,128)(2,1)}, u32[]{:S(2)}) %copy-start.1) | copy-done | bytes 2097176
  4.1 0.0 copy-start.2
  4.1 1.6 %copy-done.2 = bf16[1,512,2048]{2,1,0:T(8,128)(2,1)S(1)} copy-done((bf16[1,512,2048]{2,1,0:T(8,128)(2,1)S(1)}, bf16[1,512,2048]{2,1,0:T(8,128)(2,1)}, u32[]{:S(2)}) %copy-start.2) | copy-done | bytes 2097176
  5.7 0.0 copy-start.3
  5.7 0.0 copy-start.4
  5.7 0.0 copy-start.5
  5.7 4.6 %shard_map.93 = (f32[4,12,64,256]{3,2,1,0:T(8,128)S(1)}, bf16[4,12,64,256]{3,2,1,0:T(8,128)(2,1)S(1)}) custom-call(bf16[6144,256]{1,0:T(8,128)(2,1)S(1)} %bitcast.10, bf16[512,2048]{1,0:T(8,128)(2,1)S(1)} %bitcast.12, bf16[512,2048]{1,0:T(8,128)(2,1)S(1)} %bitcast.13), custom_call_target="tpu_custom_call" | custom-call | tf_op jit(solution)/shard_map/pallas_call | solution.py:54
  10.4 0.0 copy-done.3
  10.4 0.0 copy-done.4
  10.4 0.0 copy-done.5
  10.4 94.1 %shard_map.94 = (f32[64,256]{1,0:T(8,128)S(1)}, f32[64,256]{1,0:T(8,128)S(1)}, f32[64,256]{1,0:T(8,128)S(1)}, bf16[4,12,2,64,256]{4,3,2,1,0:T(8,128)(2,1)S(1)}) custom-call(f32[4,12,64,256]{3,2,1,0:T(8,128)S(1)} %get-tuple-element.10.keep_ref, bf16[4,12,64,256]{3,2,1,0:T(8,128)(2,1)S(1)} %get-tuple-element.11.give_ref, f32[64,256]{1,0:T(8,128)S(1)} %bitcast.14, ...), custom_call_target="tpu_custom_call" | custom-call | tf_op jit(solution)/shard_map/pallas_call | solution.py:293
  104.5 0.6 copy.14
  105.2 0.6 copy.15
  105.8 0.6 copy.16
  106.4 1.7 %copy.17 = bf16[1,6144,256]{2,1,0:T(8,128)(2,1)} copy(bf16[1,6144,256]{2,1,0:T(8,128)(2,1)S(1)} %bitcast.11) | data formatting | bytes 6291456
Async XLA Ops:
  0.6 1.9 %copy-start = (bf16[1,6144,256]{2,1,0:T(8,128)(2,1)S(1)}, bf16[1,6144,256]{2,1,0:T(8,128)(2,1)}, u32[]{:S(2)}) copy-start(bf16[1,6144,256]{2,1,0:T(8,128)(2,1)} %param.6) | copy-start | bytes 9437188
  2.5 1.6 %copy-start.1 = (bf16[1,512,2048]{2,1,0:T(8,128)(2,1)S(1)}, bf16[1,512,2048]{2,1,0:T(8,128)(2,1)}, u32[]{:S(2)}) copy-start(bf16[1,512,2048]{2,1,0:T(8,128)(2,1)} %param.7) | copy-start | bytes 6291460
  4.1 1.6 %copy-start.2 = (bf16[1,512,2048]{2,1,0:T(8,128)(2,1)S(1)}, bf16[1,512,2048]{2,1,0:T(8,128)(2,1)}, u32[]{:S(2)}) copy-start(bf16[1,512,2048]{2,1,0:T(8,128)(2,1)} %param.8) | copy-start | bytes 6291460
  5.7 4.7 %copy-start.3 = (f32[1,64,256]{2,1,0:T(8,128)S(1)}, f32[1,64,256]{2,1,0:T(8,128)}, u32[]{:S(2)}) copy-start(f32[1,64,256]{2,1,0:T(8,128)} %param.9) | copy-start | bytes 196612
  5.7 4.7 %copy-start.4 = (f32[1,64,256]{2,1,0:T(8,128)S(1)}, f32[1,64,256]{2,1,0:T(8,128)}, u32[]{:S(2)}) copy-start(f32[1,64,256]{2,1,0:T(8,128)} %param.10) | copy-start | bytes 196612
  5.7 4.7 %copy-start.5 = (f32[1,64,256]{2,1,0:T(8,128)S(1)}, f32[1,64,256]{2,1,0:T(8,128)}, u32[]{:S(2)}) copy-start(f32[1,64,256]{2,1,0:T(8,128)} %param.11) | copy-start | bytes 196612

commit v2 on v1

v2 whole, which is shorter than its diff:
```python
import jax
import jax.numpy as jnp
from jax import lax
from jax.experimental import pallas as pl
from jax.experimental.pallas import tpu as pltpu
from jax.sharding import Mesh
from jax.sharding import PartitionSpec as P

STEP = 10
NX, NZ, NC, NY = 4, 12, 2, 8
ROWS = 64
WIDTH = 256
DP = ("dp_0", "dp_1", "dp_2")
MESH = pl.DeviceIdType.MESH
REACH_REDUCE = 2
REACH_GATHER = 2
HALVES = (pl.ds(0, 32), pl.ds(32, 32))
REDUCE_ORDER = (6, 5, -5, 4, -4, 3, -3, 2, -2, 1, -1, 0)
GATHER_ORDER = (0, -1, 1, -2, 2, -3, 3, -4, 4, -5, 5, 6)
LAG = 4
LAG_A, LAG_B, LAG_C = 2, 5, 8


def relay_of(dist, reach):
    return (dist - 1) // reach * reach


def local_forward(w_hbm, x_hbm, dy_hbm, w_ref, xy_ref, a_ref, b_ref, dh_ref, d_ref, load_s):
    f32 = jnp.float32
    depth = x_hbm.shape[1]
    parts = [(x_hbm, xy_ref.at[0])]
    parts += [(w_hbm.at[pl.ds(k * depth, depth)], w_ref.at[pl.ds(k * depth, depth)]) for k in range(2)]
    parts += [(dy_hbm, xy_ref.at[1]), (w_hbm.at[pl.ds(2 * depth, depth)], w_ref.at[pl.ds(2 * depth, depth)])]
    loads = [pltpu.make_async_copy(src, dst, load_s.at[k]) for k, (src, dst) in enumerate(parts)]
    for load in loads:
        load.start()

    def compute():
        loads[0].wait()
        loads[1].wait()
        a_ref[...] = jnp.dot(xy_ref[0], w_ref[0:depth], preferred_element_type=f32)
        loads[2].wait()
        b_ref[...] = jnp.dot(xy_ref[0], w_ref[depth : 2 * depth], preferred_element_type=f32)
        loads[3].wait()
        loads[4].wait()
        dh_ref[...] = jnp.dot(xy_ref[1], w_ref[2 * depth :], preferred_element_type=f32)
        for r in range(0, a_ref.shape[0], 128):
            rows = pl.ds(r, 128)
            a, b, dh = a_ref[rows], b_ref[rows], dh_ref[rows]
            sigma = jax.nn.sigmoid(a)
            silu = a * sigma
            d_ref[0, rows] = (dh * b * sigma * (1.0 + a * (1.0 - sigma))).astype(jnp.bfloat16)
            d_ref[1, rows] = (dh * silu).astype(jnp.bfloat16)
            d_ref[2, rows] = (silu * b).astype(jnp.bfloat16)

    return compute


def step_kernel(
    w_hbm, x_hbm, dy_hbm, master_hbm, m1_hbm, m2_hbm,
    clipped_ref, all_ref,
    w_ref, xy_ref, a_ref, b_ref, dh_ref, d_ref, state_ref, keep_ref, give_ref,
    pair_buf, x1_out, x1_left, x1_right, x2_outr, x2_outl, x2_left, x2_right,
    zp_out, zm_out, zp_in, zm_in, norm_out, norm_in,
    load_s, state_s,
    pair_s, pair_r, x1_s, x1_r, x2_s, x2_r, z_s, z_r, n_s, n_r, gz_s, gz_r, gx_s, gx_r, gp_s, gp_r,
):
    f32, bf16 = jnp.float32, jnp.bfloat16
    mx, mz, mc, my = (lax.axis_index(n) for n in ("dp_0", "dp_1", "dp_2", "section"))

    def xi(k):
        return lax.rem(mx + (k + NX), NX)

    def zi(k):
        return lax.rem(mz + (k + NZ), NZ)

    def to_x(k):
        return {"dp_0": xi(k)}

    def to_z(k):
        return {"dp_1": zi(k)}

    def to_y(k):
        return {"section": lax.rem(my + (k + NY), NY)}

    partner = {"dp_2": 1 - mc}
    stages = (
        [to_z(k) for k in range(1, NZ)],
        [to_x(k) for k in range(1, NX)],
        [to_y(k) for k in range(1, NY)] + [{**to_y(k), **partner} for k in range(NY)],
    )
    peers = [device for stage in stages for device in stage]
    barrier = pltpu.get_barrier_semaphore()
    for peer in peers:
        pl.semaphore_signal(barrier, inc=1, device_id=peer, device_id_type=MESH)
    compute = local_forward(w_hbm, x_hbm, dy_hbm, w_ref, xy_ref, a_ref, b_ref, dh_ref, d_ref, load_s)
    states = [
        pltpu.make_async_copy(src, state_ref.at[k], state_s.at[k])
        for k, src in enumerate((master_hbm, m1_hbm, m2_hbm))
    ]
    for load in states:
        load.start()
    compute()

    started = []

    def send(src, dst, s, r, device):
        copy = pltpu.make_async_remote_copy(
            src_ref=src, dst_ref=dst, send_sem=s, recv_sem=r, device_id=device, device_id_type=MESH
        )
        copy.start()
        started.append(copy)
        return copy

    pair, x1, x2, zc = {}, {}, {}, {}
    per_part = x_hbm.shape[1] // 128
    low_mine = mc == 0

    def gradients(g):
        for k in range(NX):
            block = xi(k) * NZ + zi(REDUCE_ORDER[g])
            part = block // per_part
            cols = pl.multiple_of(block % per_part * 128, 128)
            rows = xy_ref[part // 2, :, pl.ds(cols, 128)]
            p = lax.dot_general(rows, d_ref[part], (((0,), (0,)), ((), ())), preferred_element_type=f32)
            low, high = p[:ROWS], p[ROWS:]
            keep_ref[g, k] = jnp.where(low_mine, low, high)
            give_ref[g, k] = jnp.where(low_mine, high, low).astype(bf16)

    def swap(g):
        pair[g] = send(give_ref.at[g], pair_buf.at[g], pair_s.at[g], pair_r.at[g], partner)

    def own(g, k):
        return keep_ref[g, k % NX] + pair_buf[g, k % NX].astype(f32)

    def first_x(g):
        pair[g].wait_recv()
        x1_out[g] = own(g, 2).astype(bf16)
        x1[g, 0] = send(x1_out.at[g, HALVES[0]], x1_left.at[g], x1_s.at[0, g], x1_r.at[0, g], to_x(1))
        x1[g, 1] = send(x1_out.at[g, HALVES[1]], x1_right.at[g], x1_s.at[1, g], x1_r.at[1, g], to_x(-1))

    def second_x(g):
        right, left = own(g, 1), own(g, -1)
        x1[g, 0].wait_recv()
        x2_outr[g, 0:32] = (right[:32] + x1_left[g].astype(f32)).astype(bf16)
        x2_outr[g, 32:64] = right[32:].astype(bf16)
        x2[g, 0] = send(x2_outr.at[g], x2_left.at[g], x2_s.at[0, g], x2_r.at[0, g], to_x(1))
        x1[g, 1].wait_recv()
        x2_outl[g, 0:32] = left[:32].astype(bf16)
        x2_outl[g, 32:64] = (left[32:] + x1_right[g].astype(f32)).astype(bf16)
        x2[g, 1] = send(x2_outl.at[g], x2_right.at[g], x2_s.at[1, g], x2_r.at[1, g], to_x(-1))

    def collect_z(way, sub, dist, value):
        arrived = (zp_in, zm_in)[way]
        for source in range(dist + 1, dist + REACH_REDUCE + 1):
            if source < 6 or (source == 6 and sub == way):
                zc[way, source, sub].wait_recv()
                value = value + arrived[source - 1, HALVES[sub]]
        return value

    def pass_z(way, dist, reduced):
        out, arrived = ((zp_out, zp_in), (zm_out, zm_in))[way]
        hops = dist - relay_of(dist, REACH_REDUCE)
        for sub, rows in enumerate(HALVES):
            if dist == 6 and sub != way:
                continue
            value = reduced[32 * sub : 32 * sub + 32]
            if dist % REACH_REDUCE == 0:
                value = collect_z(way, sub, dist, value)
            out[dist - 1, rows] = value
            zc[way, dist, sub] = send(
                out.at[dist - 1, rows], arrived.at[dist - 1, rows],
                z_s.at[way, dist - 1, sub], z_r.at[way, dist - 1, sub], to_z(hops * (1 - 2 * way)),
            )

    def third_x(g):
        off = REDUCE_ORDER[g]
        mine = own(g, 0)
        x2[g, 0].wait_recv()
        x2[g, 1].wait_recv()
        reduced = mine + x2_left[g].astype(f32) + x2_right[g].astype(f32)
        if off == 6:
            pass_z(0, 6, reduced)
            pass_z(1, 6, reduced)
        elif off > 0:
            pass_z(0, off, reduced)
        elif off < 0:
            pass_z(1, -off, reduced)
        return reduced

    count = len(REDUCE_ORDER)
    reduced = None
    gradients(0)
    pl.semaphore_wait(barrier, len(peers))
    swap(0)
    for t in range(1, count + LAG_C + 1):
        if t < count:
            gradients(t)
            swap(t)
        if 0 <= t - LAG_A < count:
            first_x(t - LAG_A)
        if 0 <= t - LAG_B < count:
            second_x(t - LAG_B)
        if 0 <= t - LAG_C < count:
            reduced = third_x(t - LAG_C)
    halves = []
    for sub in range(2):
        value = collect_z(0, sub, 0, reduced[32 * sub : 32 * sub + 32])
        halves.append(collect_z(1, sub, 0, value))
    grad = jnp.concatenate(halves, axis=0)

    part = jnp.sum(grad * grad, axis=0, keepdims=True)
    part = part[:, :128] + part[:, 128:]
    slot = 0
    for stage, devices in enumerate(stages):
        norm_out[stage] = part
        copies = []
        for device in devices:
            copies.append(send(norm_out.at[stage], norm_in.at[slot], n_s.at[slot], n_r.at[slot], device))
            slot += 1
        for k, copy in enumerate(copies):
            copy.wait_recv()
            part = part + norm_in[slot - len(copies) + k]
    total = jnp.sum(part, axis=1, keepdims=True)
    max_norm = jnp.sqrt(jnp.full((1, 1), float(NY * NX * NZ * NC * ROWS * WIDTH), f32))
    clip = jnp.minimum(1.0, max_norm / (jnp.sqrt(total) + 1e-06))
    clipped = clip * grad
    clipped_ref[...] = clipped
    for load in states:
        load.wait()
    new_master = adam(clipped, state_ref[0], state_ref[1], state_ref[2])[0]
    all_ref[mx, mz, mc] = new_master.astype(bf16)

    gz, gx, gr, gp = {}, {}, {}, {}

    def block(k, off, rows=None):
        ref = all_ref.at[xi(k), zi(off), mc]
        return ref if rows is None else ref.at[rows]

    def to_partner(g, j, k, off):
        ref = block(k, off)
        gp[g, j] = send(ref, ref, gp_s.at[g, j], gp_r.at[g, j], partner)

    def pass_on_z(way, dist, off):
        if dist % REACH_GATHER:
            return
        for target in range(dist + 1, min(dist + REACH_GATHER, 6) + 1):
            ref = block(0, off, HALVES[way] if target == 6 else None)
            gz[way, target] = send(
                ref, ref, gz_s.at[way, target - 1], gz_r.at[way, target - 1],
                to_z((target - dist) * (1 - 2 * way)),
            )

    def gather_z(g):
        off = GATHER_ORDER[g]
        if off == 0:
            pass_on_z(0, 0, 0)
            pass_on_z(1, 0, 0)
        elif off == 6:
            gz[0, 6].wait_recv()
            gz[1, 6].wait_recv()
        else:
            way, dist = (0, -off) if off < 0 else (1, off)
            gz[way, dist].wait_recv()
            pass_on_z(way, dist, off)
        ref = block(0, off)
        gx[g, 0] = send(ref, ref, gx_s.at[0, g], gx_r.at[0, g], to_x(1))
        gx[g, 1] = send(ref, ref, gx_s.at[1, g], gx_r.at[1, g], to_x(-1))
        to_partner(g, 0, 0, off)

    def gather_x(g):
        off = GATHER_ORDER[g]
        for way in range(2):
            gx[g, way].wait_recv()
            k = 2 * way - 1
            ref = block(k, off, HALVES[way])
            gr[g, way] = send(ref, ref, gx_s.at[2 + way, g], gx_r.at[2 + way, g], to_x(-k))
            to_partner(g, 1 + way, k, off)

    def gather_far(g):
        gr[g, 0].wait_recv()
        gr[g, 1].wait_recv()
        to_partner(g, 3, 2, GATHER_ORDER[g])

    for t in range(count + 2 * LAG):
        if t < count:
            gather_z(t)
        if 0 <= t - LAG < count:
            gather_x(t - LAG)
        if 0 <= t - 2 * LAG < count:
            gather_far(t - 2 * LAG)
    for copy in gp.values():
        copy.wait_recv()
    for copy in started:
        copy.wait_send()


def adam(clipped, master, moment1, moment2):
    new_m1 = 0.9 * moment1 + 0.1 * clipped
    new_m2 = 0.95 * moment2 + 0.05 * clipped * clipped
    update = new_m1 / (1.0 - 0.9**STEP) / (jnp.sqrt(new_m2 / (1.0 - 0.95**STEP)) + 1e-08) + 0.1 * master
    return master - 0.01 * update, new_m1, new_m2


def reduce_step_gather(weights, x_rows, dy_rows, master, m1, m2):
    f32, bf16 = jnp.float32, jnp.bfloat16
    vmem = pl.BlockSpec(memory_space=pltpu.VMEM)
    dma = pltpu.SemaphoreType.DMA
    tokens = x_rows.shape[0]
    blocks = pltpu.VMEM((NZ, NX, ROWS, WIDTH), bf16)
    wide = pltpu.VMEM((NZ, ROWS, WIDTH), bf16)
    half = pltpu.VMEM((NZ, ROWS // 2, WIDTH), bf16)
    ring = pltpu.VMEM((6, ROWS, WIDTH), f32)
    acts = pltpu.VMEM((tokens, WIDTH), f32)
    peers = (NX - 1) + (NZ - 1) + (2 * NY - 1)
    return pl.pallas_call(
        step_kernel,
        out_shape=(
            jax.ShapeDtypeStruct((ROWS, WIDTH), f32),
            jax.ShapeDtypeStruct((NX, NZ, NC, ROWS, WIDTH), bf16),
        ),
        in_specs=[pl.BlockSpec(memory_space=pltpu.HBM)] * 6,
        out_specs=(vmem, vmem),
        scratch_shapes=[
            pltpu.VMEM(weights.shape, bf16),
            pltpu.VMEM((2, *x_rows.shape), bf16),
            acts, acts, acts,
            pltpu.VMEM((3, tokens, WIDTH), bf16),
            pltpu.VMEM((3, ROWS, WIDTH), f32),
            pltpu.VMEM((NZ, NX, ROWS, WIDTH), f32),
            blocks, blocks,
            wide, half, half, wide, wide, wide, wide,
            ring, ring, ring, ring,
            pltpu.VMEM((3, 1, 128), f32),
            pltpu.VMEM((peers, 1, 128), f32),
            dma((5,)), dma((3,)),
            dma((NZ,)), dma((NZ,)),
            dma((2, NZ)), dma((2, NZ)),
            dma((2, NZ)), dma((2, NZ)),
            dma((2, 6, 2)), dma((2, 6, 2)),
            dma((peers,)), dma((peers,)),
            dma((2, 6)), dma((2, 6)),
            dma((4, NZ)), dma((4, NZ)),
            dma((NZ, 4)), dma((NZ, 4)),
        ],
        compiler_params=pltpu.CompilerParams(
            collective_id=0, has_side_effects=True, vmem_limit_bytes=34 << 20
        ),
    )(*(pltpu.with_memory_space_constraint(v, pltpu.HBM) for v in (weights, x_rows, dy_rows, master, m1, m2)))


def local(weights, inputs, out_grads, master, moment1, moment2):
    clipped, gathered = reduce_step_gather(
        weights[0], inputs[0], out_grads[0], master[0], moment1[0], moment2[0]
    )
    outs = adam(clipped[None], master, moment1, moment2)
    return (*outs, gathered.reshape(weights.shape))


def solution(mesh):
    split = Mesh(
        mesh.devices.reshape(NX, NZ, NC, mesh.shape["section"]), ("dp_0", "dp_1", "dp_2", "section")
    )
    shard = P("section", DP, None)
    whole = P("section", None, None)
    return jax.shard_map(
        local,
        mesh=split,
        in_specs=(whole, shard, shard, shard, shard, shard),
        out_specs=(shard, shard, shard, whole),
        check_vma=False,
    )
```

time: 108 us -> 88.6 us (0.82)
  Pallas kernels: 98.8 us -> 85.4 us
  local copies, waits for them, and re-layouts: 8.63 us -> 1.68 us
    pallas_call x2 -> x1, Pallas kernels: 98.8 us -> 85.4 us  [reduce_step_gather(): pl.pallas_call(step_kernel, out_shape=(jax.ShapeDtypeStruct((ROWS, WIDTH)...]
    unnamed x16 -> x7, local copies, waits for them, and re-layouts: 8.63 us -> 1.68 us
where the time goes in v2:
time: 88.6 us; the launch traced here: 88.4 us
  Pallas kernels  85.4 us (96%)
  local copies, waits for them, and re-layouts  1.68 us (2%)
    pallas_call x1, Pallas kernels, reduce_step_gather(): pl.pallas_call(step_kernel, out_shape=(jax.ShapeDtypeStruct((ROWS, WIDTH)...  85.4 us

profile of v2, /device:TPU:1, one launch (start us, length us, event | category | flops | bytes accessed | tf_op | source)
XLA Modules:
  0.0 88.4 jit_solution(7215272227027231251)
XLA Ops:
  0.6 0.0 copy-start
  0.6 0.0 copy-start.1
  0.7 0.0 copy-start.2
  0.7 85.4 %shard_map.93 = (f32[64,256]{1,0:T(8,128)S(1)}, bf16[4,12,2,64,256]{4,3,2,1,0:T(8,128)(2,1)S(1)}) custom-call(bf16[6144,256]{1,0:T(8,128)(2,1)} %bitcast.16, bf16[512,2048]{1,0:T(8,128)(2,1)} %bitcast.17, bf16[512,2048]{1,0:T(8,128)(2,1)} %bitcast.18, f32[64,256]{1,0:T(8,128)} %bitcast.19, f32[64,256]{1,0:T(8,128)} %bitcast.20, f32[64,256]{1,0:T(8,128)} %bitcast.21), custom_call_target="tpu_custom_call" | custom-call | tf_op jit(solution)/shard_map/pallas_call | solution.py:316
  86.1 0.0 copy-done
  86.1 0.0 copy-done.1
  86.1 0.0 copy-done.2
  86.1 0.7 multiply_subtract_fusion
  86.8 1.7 %copy.11 = bf16[1,6144,256]{2,1,0:T(8,128)(2,1)} copy(bf16[1,6144,256]{2,1,0:T(8,128)(2,1)S(1)} %bitcast.15) | data formatting | bytes 6291456
Async XLA Ops:
  0.6 85.4 %copy-start = (f32[1,64,256]{2,1,0:T(8,128)S(1)}, f32[1,64,256]{2,1,0:T(8,128)}, u32[]{:S(2)}) copy-start(f32[1,64,256]{2,1,0:T(8,128)} %param.9) | copy-start | bytes 196612
  0.6 85.4 %copy-start.1 = (f32[1,64,256]{2,1,0:T(8,128)S(1)}, f32[1,64,256]{2,1,0:T(8,128)}, u32[]{:S(2)}) copy-start(f32[1,64,256]{2,1,0:T(8,128)} %param.10) | copy-start | bytes 196612
  0.7 85.4 %copy-start.2 = (f32[1,64,256]{2,1,0:T(8,128)S(1)}, f32[1,64,256]{2,1,0:T(8,128)}, u32[]{:S(2)}) copy-start(f32[1,64,256]{2,1,0:T(8,128)} %param.11) | copy-start | bytes 196612

commit v3 on v2

--- a/solution.py
+++ b/solution.py
@@ -7,13 +7,14 @@
 from jax.sharding import PartitionSpec as P
 
 STEP = 10
+CHUNKS = 4
 NX, NZ, NC, NY = 4, 12, 2, 8
 ROWS = 64
 WIDTH = 256
 DP = ("dp_0", "dp_1", "dp_2")
 MESH = pl.DeviceIdType.MESH
 REACH_REDUCE = 2
-REACH_GATHER = 2
+REACH_GATHER = 3
 HALVES = (pl.ds(0, 32), pl.ds(32, 32))
 REDUCE_ORDER = (6, 5, -5, 4, -4, 3, -3, 2, -2, 1, -1, 0)
 GATHER_ORDER = (0, -1, 1, -2, 2, -3, 3, -4, 4, -5, 5, 6)
@@ -26,32 +27,57 @@
 
 
 def local_forward(w_hbm, x_hbm, dy_hbm, w_ref, xy_ref, a_ref, b_ref, dh_ref, d_ref, load_s):
-    f32 = jnp.float32
+    f32, bf16 = jnp.float32, jnp.bfloat16
     depth = x_hbm.shape[1]
-    parts = [(x_hbm, xy_ref.at[0])]
-    parts += [(w_hbm.at[pl.ds(k * depth, depth)], w_ref.at[pl.ds(k * depth, depth)]) for k in range(2)]
-    parts += [(dy_hbm, xy_ref.at[1]), (w_hbm.at[pl.ds(2 * depth, depth)], w_ref.at[pl.ds(2 * depth, depth)])]
-    loads = [pltpu.make_async_copy(src, dst, load_s.at[k]) for k, (src, dst) in enumerate(parts)]
-    for load in loads:
-        load.start()
+    tile = depth // CHUNKS
+    loads = []
+
+    def load(src, dst):
+        copy = pltpu.make_async_copy(src, dst, load_s.at[len(loads)])
+        copy.start()
+        loads.append(copy)
+        return copy
+
+    first, second = [], []
+    for k in range(CHUNKS):
+        cols = pl.ds(k * tile, tile)
+        waits = [load(x_hbm.at[:, cols], xy_ref.at[0, :, cols])]
+        for part in range(2):
+            rows = pl.ds(part * depth + k * tile, tile)
+            waits.append(load(w_hbm.at[rows], w_ref.at[rows]))
+        first.append(waits)
+    for k in range(CHUNKS):
+        cols, rows = pl.ds(k * tile, tile), pl.ds(2 * depth + k * tile, tile)
+        second.append([load(dy_hbm.at[:, cols], xy_ref.at[1, :, cols]), load(w_hbm.at[rows], w_ref.at[rows])])
+
+    def accumulate(out_ref, which, k, part):
+        cols, rows = pl.ds(k * tile, tile), pl.ds(part * depth + k * tile, tile)
+        product = jnp.dot(xy_ref[which, :, cols], w_ref[rows], preferred_element_type=f32)
+        out_ref[...] = product if k == 0 else out_ref[...] + product
 
     def compute():
-        loads[0].wait()
-        loads[1].wait()
-        a_ref[...] = jnp.dot(xy_ref[0], w_ref[0:depth], preferred_element_type=f32)
-        loads[2].wait()
-        b_ref[...] = jnp.dot(xy_ref[0], w_ref[depth : 2 * depth], preferred_element_type=f32)
-        loads[3].wait()
-        loads[4].wait()
-        dh_ref[...] = jnp.dot(xy_ref[1], w_ref[2 * depth :], preferred_element_type=f32)
+        for k in range(CHUNKS):
+            for copy in first[k]:
+                copy.wait()
+            accumulate(a_ref, 0, k, 0)
+            accumulate(b_ref, 0, k, 1)
         for r in range(0, a_ref.shape[0], 128):
             rows = pl.ds(r, 128)
-            a, b, dh = a_ref[rows], b_ref[rows], dh_ref[rows]
+            a, b = a_ref[rows], b_ref[rows]
             sigma = jax.nn.sigmoid(a)
             silu = a * sigma
-            d_ref[0, rows] = (dh * b * sigma * (1.0 + a * (1.0 - sigma))).astype(jnp.bfloat16)
-            d_ref[1, rows] = (dh * silu).astype(jnp.bfloat16)
-            d_ref[2, rows] = (silu * b).astype(jnp.bfloat16)
+            d_ref[2, rows] = (silu * b).astype(bf16)
+            a_ref[rows] = silu
+            b_ref[rows] = b * sigma * (1.0 + a * (1.0 - sigma))
+        for k in range(CHUNKS):
+            for copy in second[k]:
+                copy.wait()
+            accumulate(dh_ref, 1, k, 2)
+        for r in range(0, a_ref.shape[0], 128):
+            rows = pl.ds(r, 128)
+            dh = dh_ref[rows]
+            d_ref[0, rows] = (dh * b_ref[rows]).astype(bf16)
+            d_ref[1, rows] = (dh * a_ref[rows]).astype(bf16)
 
     return compute
 
@@ -68,11 +94,15 @@
     f32, bf16 = jnp.float32, jnp.bfloat16
     mx, mz, mc, my = (lax.axis_index(n) for n in ("dp_0", "dp_1", "dp_2", "section"))
 
+    xs = [lax.rem(mx + k, NX) for k in range(NX)]
+    zs = [lax.rem(mz + k, NZ) for k in range(NZ)]
+    ys = [lax.rem(my + k, NY) for k in range(NY)]
+
     def xi(k):
-        return lax.rem(mx + (k + NX), NX)
+        return xs[k % NX]
 
     def zi(k):
-        return lax.rem(mz + (k + NZ), NZ)
+        return zs[k % NZ]
 
     def to_x(k):
         return {"dp_0": xi(k)}
@@ -81,13 +111,12 @@
         return {"dp_1": zi(k)}
 
     def to_y(k):
-        return {"section": lax.rem(my + (k + NY), NY)}
+        return {"section": ys[k]}
 
     partner = {"dp_2": 1 - mc}
     stages = (
-        [to_z(k) for k in range(1, NZ)],
-        [to_x(k) for k in range(1, NX)],
-        [to_y(k) for k in range(1, NY)] + [{**to_y(k), **partner} for k in range(NY)],
+        [to_z(k) for k in range(1, NZ)] + [{**to_z(k), **partner} for k in range(NZ)],
+        [{**to_x(j), **to_y(k)} for j in range(NX) for k in range(NY) if j or k],
     )
     peers = [device for stage in stages for device in stage]
     barrier = pltpu.get_barrier_semaphore()
@@ -119,9 +148,9 @@
     def gradients(g):
         for k in range(NX):
             block = xi(k) * NZ + zi(REDUCE_ORDER[g])
-            part = block // per_part
-            cols = pl.multiple_of(block % per_part * 128, 128)
-            rows = xy_ref[part // 2, :, pl.ds(cols, 128)]
+            part = lax.div(block, per_part)
+            cols = pl.multiple_of(lax.rem(block, per_part) * 128, 128)
+            rows = xy_ref[lax.div(part, 2), :, pl.ds(cols, 128)]
             p = lax.dot_general(rows, d_ref[part], (((0,), (0,)), ((), ())), preferred_element_type=f32)
             low, high = p[:ROWS], p[ROWS:]
             keep_ref[g, k] = jnp.where(low_mine, low, high)
@@ -229,13 +258,15 @@
     for load in states:
         load.wait()
     new_master = adam(clipped, state_ref[0], state_ref[1], state_ref[2])[0]
-    all_ref[mx, mz, mc] = new_master.astype(bf16)
-
-    gz, gx, gr, gp = {}, {}, {}, {}
+    all_ref[(mx * NZ + mz) * NC + mc] = new_master.astype(bf16)
+
+    gz, gx, gr, gp, places = {}, {}, {}, {}, {}
 
     def block(k, off, rows=None):
-        ref = all_ref.at[xi(k), zi(off), mc]
-        return ref if rows is None else ref.at[rows]
+        key = k % NX, off % NZ
+        if key not in places:
+            places[key] = (xi(k) * NZ + zi(off)) * NC + mc
+        return all_ref.at[places[key]] if rows is None else all_ref.at[places[key], rows]
 
     def to_partner(g, j, k, off):
         ref = block(k, off)
@@ -312,12 +343,12 @@
     half = pltpu.VMEM((NZ, ROWS // 2, WIDTH), bf16)
     ring = pltpu.VMEM((6, ROWS, WIDTH), f32)
     acts = pltpu.VMEM((tokens, WIDTH), f32)
-    peers = (NX - 1) + (NZ - 1) + (2 * NY - 1)
+    peers = (NC * NZ - 1) + (NX * NY - 1)
     return pl.pallas_call(
         step_kernel,
         out_shape=(
             jax.ShapeDtypeStruct((ROWS, WIDTH), f32),
-            jax.ShapeDtypeStruct((NX, NZ, NC, ROWS, WIDTH), bf16),
+            jax.ShapeDtypeStruct((NX * NZ * NC, ROWS, WIDTH), bf16),
         ),
         in_specs=[pl.BlockSpec(memory_space=pltpu.HBM)] * 6,
         out_specs=(vmem, vmem),
@@ -333,7 +364,7 @@
             ring, ring, ring, ring,
             pltpu.VMEM((3, 1, 128), f32),
             pltpu.VMEM((peers, 1, 128), f32),
-            dma((5,)), dma((3,)),
+            dma((5 * CHUNKS,)), dma((3,)),
             dma((NZ,)), dma((NZ,)),
             dma((2, NZ)), dma((2, NZ)),
             dma((2, NZ)), dma((2, NZ)),

time: 88.6 us -> 86.1 us (0.972)
  Pallas kernels: 85.4 us -> 82.9 us
    pallas_call x1, Pallas kernels: 85.4 us -> 82.9 us  [reduce_step_gather(): pl.pallas_call(step_kernel, out_shape=(jax.ShapeDtypeStruct((ROWS, WIDTH)...]
where the time goes in v3:
time: 86.1 us; the launch traced here: 85.9 us
  Pallas kernels  82.9 us (96%)
  local copies, waits for them, and re-layouts  1.68 us (2%)
    pallas_call x1, Pallas kernels, reduce_step_gather(): pl.pallas_call(step_kernel, out_shape=(jax.ShapeDtypeStruct((ROWS, WIDTH)...  82.9 us

profile of v3, /device:TPU:1, one launch (start us, length us, event | category | flops | bytes accessed | tf_op | source)
XLA Modules:
  0.0 85.9 jit_solution(3144196478557977339)
XLA Ops:
  0.6 0.0 copy-start
  0.6 0.0 copy-start.1
  0.7 0.0 copy-start.2
  0.7 82.9 %shard_map.93 = (f32[64,256]{1,0:T(8,128)S(1)}, bf16[96,64,256]{2,1,0:T(8,128)(2,1)S(1)}) custom-call(bf16[6144,256]{1,0:T(8,128)(2,1)} %bitcast.16, bf16[512,2048]{1,0:T(8,128)(2,1)} %bitcast.17, bf16[512,2048]{1,0:T(8,128)(2,1)} %bitcast.18, f32[64,256]{1,0:T(8,128)} %bitcast.19, f32[64,256]{1,0:T(8,128)} %bitcast.20, f32[64,256]{1,0:T(8,128)} %bitcast.21), custom_call_target="tpu_custom_call" | custom-call | tf_op jit(solution)/shard_map/pallas_call | solution.py:347
  83.6 0.0 copy-done
  83.6 0.0 copy-done.1
  83.6 0.0 copy-done.2
  83.6 0.7 multiply_subtract_fusion
  84.3 1.7 %copy.11 = bf16[1,6144,256]{2,1,0:T(8,128)(2,1)} copy(bf16[1,6144,256]{2,1,0:T(8,128)(2,1)S(1)} %bitcast.15) | data formatting | bytes 6291456
Async XLA Ops:
  0.6 82.9 %copy-start = (f32[1,64,256]{2,1,0:T(8,128)S(1)}, f32[1,64,256]{2,1,0:T(8,128)}, u32[]{:S(2)}) copy-start(f32[1,64,256]{2,1,0:T(8,128)} %param.9) | copy-start | bytes 196612
  0.6 82.9 %copy-start.1 = (f32[1,64,256]{2,1,0:T(8,128)S(1)}, f32[1,64,256]{2,1,0:T(8,128)}, u32[]{:S(2)}) copy-start(f32[1,64,256]{2,1,0:T(8,128)} %param.10) | copy-start | bytes 196612
  0.7 82.9 %copy-start.2 = (f32[1,64,256]{2,1,0:T(8,128)S(1)}, f32[1,64,256]{2,1,0:T(8,128)}, u32[]{:S(2)}) copy-start(f32[1,64,256]{2,1,0:T(8,128)} %param.11) | copy-start | bytes 196612
